TPU v7x, 32 devices: a whole 2x2x4 slice. The times are simulated.
32 devices in a mesh: gx: 4 (over y, x), gy: 8 (over z, core).
Axes of the slice: x: 2, y: 2, z: 4, core: 2. Of those that a mesh axis runs over, the one named last changes fastest.
Arguments:
- schur: float32 [4, 8, 512, 512], P('gx', 'gy'), may hold values from -1 to 25, as said below
- precond: float32 [4, 8, 512, 512], P('gx', 'gy'), may hold values from -1 to 25, as said below
- loads: float32 [4, 8, 512, 256], P('gx', 'gy'), may hold values from -12 to 12
- coarse_inv: float32 [128, 128], P('gx'), may hold values from -1 to 25, as said below
- edge_rows: int32 [4, 8, 512], P('gx', 'gy'), may hold values from 0 to 511, each once within a row
- corner_rows: int32 [4, 8, 4], P('gx', 'gy'), may hold values from 0 to 511, as said below
Outputs:
- multipliers: float32 [4, 8, 512, 256], P('gx', 'gy')
- residual: float32 [4, 8, 512, 256], P('gx', 'gy')
Inputs may be any that keep to these rules, and one draw needn't show every extreme that they name: `edge_rows`: for every subdomain the 512 entries name each local interface row once. `corner_rows`: local interface rows of each subdomain's 4 corner modes; entries of one subdomain may repeat. `schur`: every subdomain's block is symmetric positive definite. `precond`: every subdomain's block is symmetric positive definite. `coarse_inv`: symmetric positive definite; row and column (i * 8 + j) * 4 + m belong to mode m of subdomain (i, j).
All inputs are finite; a program needn't handle non-finite values.
Results may differ from a plain program's by a relative error of at most 0.00017.
Values sent between devices are 32-bit elements; how exact they have to be, the bound alone decides.
No kernel may reach another device: no remote copies, remote signals or barrier semaphores. Data moves between devices by JAX's collectives and lax.ppermute only.
A program may use at most 64 MiB of HBM per device.

v0:
```python
import jax
import jax.numpy as jnp
from jax import lax
from jax.sharding import PartitionSpec as P

MODES = 4
ITERS = 2
highest = lax.Precision.HIGHEST


def with_halo(cells, sides, width):
    for axis, dim in sides:
        count = lax.axis_size(axis)
        head = lax.slice_in_dim(cells, 0, width, axis=dim)
        tail = lax.slice_in_dim(cells, cells.shape[dim] - width, cells.shape[dim], axis=dim)
        cells = jnp.concatenate(
            [
                lax.ppermute(tail, axis, [(i, (i + 1) % count) for i in range(count)]),
                cells,
                lax.ppermute(head, axis, [((i + 1) % count, i) for i in range(count)]),
            ],
            axis=dim,
        )
    return cells


def matmul(first_op, second_op):
    return jnp.dot(first_op, second_op, precision=highest, preferred_element_type=jnp.float32)


def edge_jumps(source, local_rows, inverse):
    edge_size = local_rows.shape[0] // 4
    picked = jnp.take(source, local_rows, axis=0).reshape(4, edge_size, source.shape[1])
    across = with_halo(picked[0:2], (("gx", 0),), 1)
    upward = with_halo(picked[2:4], (("gy", 0),), 1)
    west_jump = picked[0] - across[0]
    east_jump = picked[1] - across[3]
    south_jump = picked[2] - upward[0]
    north_jump = picked[3] - upward[3]
    stacked = jnp.stack([west_jump, east_jump, south_jump, north_jump]).reshape(source.shape)
    return jnp.take(stacked, inverse, axis=0)


def coarse_by_column(corner_res, coarse_inv, grid_row):
    across_count = lax.axis_size("gx")
    along_count = lax.axis_size("gy")
    column_res = lax.all_gather(corner_res, "gx", axis=0, tiled=True)
    group_rows = coarse_inv.shape[0]
    shaped = coarse_inv.reshape(group_rows, across_count, along_count, MODES)
    chosen = lax.dynamic_slice_in_dim(shaped, grid_row, 1, 2).reshape(
        group_rows, across_count * MODES
    )
    return lax.psum_scatter(matmul(chosen, column_res), "gy", scatter_dimension=0, tiled=True)


def on_device(schur, precond, loads, coarse_inv, edge_rows, corner_rows):
    schur_block = schur[0, 0]
    precond_block = precond[0, 0]
    local_loads = loads[0, 0]
    local_rows = edge_rows[0, 0]
    corner_local = corner_rows[0, 0]
    row_total = local_rows.shape[0]
    positions = jnp.arange(row_total, dtype=jnp.int32)
    inverse = jnp.zeros((row_total,), jnp.int32).at[local_rows].set(positions)
    corner_pick = (corner_local[:, None] == positions[None, :]).astype(jnp.float32)
    grid_row = lax.axis_index("gy")
    dual_rhs = edge_jumps(local_loads, local_rows, inverse)
    multipliers = jnp.zeros_like(dual_rhs)
    residual = dual_rhs
    for iteration in range(ITERS):
        corner_res = matmul(corner_pick, residual)
        coarse_sol = coarse_by_column(corner_res, coarse_inv, grid_row)
        lifted = 0.25 * matmul(precond_block, residual) + matmul(corner_pick.T, coarse_sol)
        search = edge_jumps(lifted, local_rows, inverse)
        schur_image = matmul(schur_block, search)
        numerator = lax.psum(jnp.sum(residual * search, axis=0), ("gx", "gy"))
        dual_image = edge_jumps(schur_image, local_rows, inverse)
        denominator = lax.psum(jnp.sum(search * dual_image, axis=0), ("gx", "gy"))
        step_size = numerator / denominator
        multipliers = multipliers + step_size * search
        residual = residual - step_size * dual_image
    return (multipliers[None, None], residual[None, None])


def solution(mesh):
    in_specs = (
        P("gx", "gy", None, None),
        P("gx", "gy", None, None),
        P("gx", "gy", None, None),
        P("gx", None),
        P("gx", "gy", None),
        P("gx", "gy", None),
    )
    out_specs = (P("gx", "gy", None, None), P("gx", "gy", None, None))
    return jax.shard_map(
        on_device, mesh=mesh, in_specs=in_specs, out_specs=out_specs, check_vma=False
    )
```

profile of v0, /device:TPU:10, one launch (start us, length us, event | category | flops | bytes accessed | tf_op | source)
XLA Modules:
  0.0 237.9 jit_solution(15812877509895643523)
XLA Ops:
  1.5 2.6 %gather_fusion = f32[512,256]{1,0:T(8,128)S(1)} fusion(f32[512,256]{1,0:T(8,128)} %bitcast.136, s32[1024]{0:T(1024)S(1)} %pad_clamp_fusion.1), kind=kCustom, calls=%fused_computation.clone | custom fusion | bytes 1050624 | tf_op jit(solution)/shard_map/jit(_take)/gather | solution.py:33
  5.8 1.7 collective-permute-start.3
  8.1 2.4 %scatter_custom_fusion = s32[512]{0:T(512)S(1)} fusion(s32[512]{0:T(512)S(1)} %bitcast.146, s32[512]{0:T(512)S(1)} %iota.6, s32[]{:T(128)} %constant.1.clone.1), kind=kCustom, calls=%fused_computation.90 | custom fusion | bytes 2052 | tf_op jit(solution)/shard_map/scatter | solution.py:64
  13.9 1.6 gather_fusion.1
  16.5 7.2 %all-gather = f32[4,4,256]{2,1,0:T(4,128)S(1)} all-gather(f32[1,4,256]{2,1,0:T(4,128)S(1)} %convolution_bitcast_fusion.3), channel_id=1, replica_groups=mesh['gx'=4,'gy'=8] {'gx'}, dimensions={0}, use_global_device_ids=true | all-gather | bytes 20480 | tf_op jit(solution)/shard_map/all_gather | solution.py:47
  24.0 24.0 %all-reduce = f32[32,256]{1,0:T(8,128)S(1)} all-reduce(f32[32,256]{1,0:T(8,128)S(1)} %fusion.56), channel_id=2, replica_groups=mesh['gx'=4,'gy'=8] {'gy'}, use_global_device_ids=true, to_apply=%region_1.0.clone | all-reduce | flops 8192 | bytes 65536
  48.5 2.0 fusion.2
  50.6 1.6 gather_fusion.2
  53.9 1.7 collective-permute-start.7
  58.3 3.2 %collective-permute-done.5 = f32[1,128,256]{2,1,0:T(8,128)S(1)} collective-permute-done((f32[1,128,256]{2,1,0:T(8,128)S(1)}, f32[1,128,256]{2,1,0:T(8,128)S(1)}, u32[]{:S(2)}, u32[]{:S(2)}) %collective-permute-start.5) | collective-permute-done | bytes 131104 | tf_op jit(solution)/shard_map/ppermute | solution.py:20
  61.6 1.6 gather_fusion.3
  63.2 3.2 %convolution_bitcast_fusion.1 = f32[512,256]{0,1:T(8,128)S(1)} fusion(f32[1,1,512,512]{3,2,1,0:T(8,128)} %param.8, f32[512,256]{1,0:T(8,128)S(1)} %gather_fusion.3, pred[512]{0:T(512)(128)(4,1)S(1)} %compare_and_fusion), kind=kOutput, calls=%fused_computation.18 | convolution fusion | flops 805437440 | bytes 2097664 | tf_op jit(solution)/shard_map/dot_general | solution.py:28
  66.6 1.6 gather_fusion.4
  69.5 2.1 collective-permute-start.11
  72.2 2.0 collective-permute-done.8
  74.2 3.2 %collective-permute-done.9 = f32[1,128,256]{2,1,0:T(8,128)S(1)} collective-permute-done((f32[1,128,256]{2,1,0:T(8,128)S(1)}, f32[1,128,256]{2,1,0:T(8,128)S(1)}, u32[]{:S(2)}, u32[]{:S(2)}) %collective-permute-start.9) | collective-permute-done | bytes 131104 | tf_op jit(solution)/shard_map/ppermute | solution.py:20
  77.6 1.6 gather_fusion.5
  79.4 45.9 %all-reduce.3 = (f32[256]{0:T(256)S(1)}, f32[256]{0:T(256)S(1)}) all-reduce(f32[256]{0:T(256)S(1)} %get-tuple-element.6, f32[256]{0:T(256)S(1)} %get-tuple-element.5), channel_id=1, replica_groups=mesh['gx'=4,'gy'=8] {'gx','gy'}, use_global_device_ids=true, to_apply=%region_3.5 | all-reduce | flops 512 | bytes 4096 | tf_op jit(solution)/shard_map/psum | solution.py:76
  125.7 7.8 %all-gather.1 = f32[4,4,256]{2,1,0:T(4,128)S(1)} all-gather(f32[1,4,256]{2,1,0:T(4,128)S(1)} %convolution_bitcast_fusion.2), channel_id=1, replica_groups=mesh['gx'=4,'gy'=8] {'gx'}, dimensions={0}, use_global_device_ids=true | all-gather | bytes 20480 | tf_op jit(solution)/shard_map/all_gather | solution.py:47
  133.8 21.0 %all-reduce.1 = f32[32,256]{1,0:T(8,128)S(1)} all-reduce(f32[32,256]{1,0:T(8,128)S(1)} %fusion.57), channel_id=3, replica_groups=mesh['gx'=4,'gy'=8] {'gy'}, use_global_device_ids=true, to_apply=%region_6.8.clone | all-reduce | flops 8192 | bytes 65536
  155.2 1.9 fusion.3
  157.3 1.6 gather_fusion.6
  160.6 1.7 collective-permute-start.15
  165.0 3.2 %collective-permute-done.13 = f32[1,128,256]{2,1,0:T(8,128)S(1)} collective-permute-done((f32[1,128,256]{2,1,0:T(8,128)S(1)}, f32[1,128,256]{2,1,0:T(8,128)S(1)}, u32[]{:S(2)}, u32[]{:S(2)}) %collective-permute-start.13) | collective-permute-done | bytes 131104 | tf_op jit(solution)/shard_map/ppermute | solution.py:20
  168.3 1.6 gather_fusion.7
  169.9 4.0 %convolution_bitcast_fusion = f32[512,256]{0,1:T(8,128)} fusion(f32[1,1,512,512]{3,2,1,0:T(8,128)} %param.8, f32[512,256]{1,0:T(8,128)S(1)} %gather_fusion.7, pred[512]{0:T(512)(128)(4,1)S(1)} %compare_and_fusion), kind=kOutput, calls=%fused_computation.17 | convolution fusion | flops 805437440 | bytes 2097664 | tf_op jit(solution)/shard_map/dot_general | solution.py:28
  175.1 2.2 gather_fusion.8
  179.2 2.1 collective-permute-start.19
  182.4 2.0 collective-permute-done.16
  184.4 2.7 %collective-permute-done.17 = f32[1,128,256]{2,1,0:T(8,128)S(1)} collective-permute-done((f32[1,128,256]{2,1,0:T(8,128)S(1)}, f32[1,128,256]{2,1,0:T(8,128)S(1)}, u32[]{:S(2)}, u32[]{:S(2)}) %collective-permute-start.17) | collective-permute-done | bytes 131104 | tf_op jit(solution)/shard_map/ppermute | solution.py:20
  187.3 2.2 gather_fusion.9
  190.8 45.9 %all-reduce.2 = (f32[256]{0:T(256)S(1)}, f32[256]{0:T(256)S(1)}) all-reduce(f32[256]{0:T(256)S(1)} %get-tuple-element.4, f32[256]{0:T(256)S(1)} %get-tuple-element.3), channel_id=1, replica_groups=mesh['gx'=4,'gy'=8] {'gx','gy'}, use_global_device_ids=true, to_apply=%region_8.10 | all-reduce | flops 512 | bytes 4096 | tf_op jit(solution)/shard_map/psum | solution.py:76
  (90 shorter events, 27.0 us)
Async XLA Ops:
  0.6 47.8 %copy-start = (f32[1,1,512,512]{3,2,1,0:T(8,128)S(1)}, f32[1,1,512,512]{3,2,1,0:T(8,128)}, u32[]{:S(2)}) copy-start(f32[1,1,512,512]{3,2,1,0:T(8,128)} %param.9) | copy-start | bytes 3145732
  0.6 0.8 copy-start.2
  4.3 8.4 %collective-permute-start = (f32[1,128,256]{2,1,0:T(8,128)S(1)}, f32[1,128,256]{2,1,0:T(8,128)S(1)}, u32[]{:S(2)}, u32[]{:S(2)}) collective-permute-start(f32[1,128,256]{2,1,0:T(8,128)S(1)} %get-tuple-element.47), channel_id=1, source_target_pairs={{0,8},{8,16},{16,24},{24,0},{1,9},{9,17},{17,25},{25,1},{2,10},{10... | collective-permute-start | bytes 393224 | tf_op jit(solution)/shard_map/ppermute | solution.py:18
  5.8 6.8 %collective-permute-start.2 = (f32[1,128,256]{2,1,0:T(8,128)S(1)}, f32[1,128,256]{2,1,0:T(8,128)S(1)}, u32[]{:S(2)}, u32[]{:S(2)}) collective-permute-start(f32[1,128,256]{2,1,0:T(8,128)S(1)} %get-tuple-element.48), channel_id=1, source_target_pairs={{0,1},{1,2},{2,3},{3,4},{4,5},{5,6},{6,7},{7,0},{8,9},{9,10},{10,1... | collective-permute-start | bytes 393224 | tf_op jit(solution)/shard_map/ppermute | solution.py:18
  5.8 6.8 %collective-permute-start.3 = (f32[1,128,256]{2,1,0:T(8,128)S(1)}, f32[1,128,256]{2,1,0:T(8,128)S(1)}, u32[]{:S(2)}, u32[]{:S(2)}) collective-permute-start(f32[1,128,256]{2,1,0:T(8,128)S(1)} %get-tuple-element.49), channel_id=1, source_target_pairs={{1,0},{2,1},{3,2},{4,3},{5,4},{6,5},{7,6},{0,7},{9,8},{10,9},{11,1... | collective-permute-start | bytes 393224 | tf_op jit(solution)/shard_map/ppermute | solution.py:20
  7.6 6.2 %collective-permute-start.1 = (f32[1,128,256]{2,1,0:T(8,128)S(1)}, f32[1,128,256]{2,1,0:T(8,128)S(1)}, u32[]{:S(2)}, u32[]{:S(2)}) collective-permute-start(f32[1,128,256]{2,1,0:T(8,128)S(1)} %get-tuple-element.50), channel_id=1, source_target_pairs={{8,0},{16,8},{24,16},{0,24},{9,1},{17,9},{25,17},{1,25},{10,2},{18... | collective-permute-start | bytes 393224 | tf_op jit(solution)/shard_map/ppermute | solution.py:20
  8.1 2.5 %copy-start.3 = (f32[32,128]{1,0:T(8,128)S(1)}, f32[32,128]{1,0:T(8,128)}, u32[]{:S(2)}) copy-start(f32[32,128]{1,0:T(8,128)} %param.11) | copy-start | bytes 49156
  10.7 0.7 copy-start.5
  15.5 0.7 copy-start.4
  52.4 5.3 %collective-permute-start.4 = (f32[1,128,256]{2,1,0:T(8,128)S(1)}, f32[1,128,256]{2,1,0:T(8,128)S(1)}, u32[]{:S(2)}, u32[]{:S(2)}) collective-permute-start(f32[1,128,256]{2,1,0:T(8,128)S(1)} %get-tuple-element.39), channel_id=1, source_target_pairs={{0,8},{8,16},{16,24},{24,0},{1,9},{9,17},{17,25},{25,1},{2,10},{10... | collective-permute-start | bytes 393224 | tf_op jit(solution)/shard_map/ppermute | solution.py:18
  53.9 4.4 %collective-permute-start.6 = (f32[1,128,256]{2,1,0:T(8,128)S(1)}, f32[1,128,256]{2,1,0:T(8,128)S(1)}, u32[]{:S(2)}, u32[]{:S(2)}) collective-permute-start(f32[1,128,256]{2,1,0:T(8,128)S(1)} %get-tuple-element.40), channel_id=1, source_target_pairs={{0,1},{1,2},{2,3},{3,4},{4,5},{5,6},{6,7},{7,0},{8,9},{9,10},{10,1... | collective-permute-start | bytes 393224 | tf_op jit(solution)/shard_map/ppermute | solution.py:18
  53.9 4.4 %collective-permute-start.7 = (f32[1,128,256]{2,1,0:T(8,128)S(1)}, f32[1,128,256]{2,1,0:T(8,128)S(1)}, u32[]{:S(2)}, u32[]{:S(2)}) collective-permute-start(f32[1,128,256]{2,1,0:T(8,128)S(1)} %get-tuple-element.41), channel_id=1, source_target_pairs={{1,0},{2,1},{3,2},{4,3},{5,4},{6,5},{7,6},{0,7},{9,8},{10,9},{11,1... | collective-permute-start | bytes 393224 | tf_op jit(solution)/shard_map/ppermute | solution.py:20
  55.7 5.9 %collective-permute-start.5 = (f32[1,128,256]{2,1,0:T(8,128)S(1)}, f32[1,128,256]{2,1,0:T(8,128)S(1)}, u32[]{:S(2)}, u32[]{:S(2)}) collective-permute-start(f32[1,128,256]{2,1,0:T(8,128)S(1)} %get-tuple-element.42), channel_id=1, source_target_pairs={{8,0},{16,8},{24,16},{0,24},{9,1},{17,9},{25,17},{1,25},{10,2},{18... | collective-permute-start | bytes 393224 | tf_op jit(solution)/shard_map/ppermute | solution.py:20
  68.4 5.8 %collective-permute-start.8 = (f32[1,128,256]{2,1,0:T(8,128)S(1)}, f32[1,128,256]{2,1,0:T(8,128)S(1)}, u32[]{:S(2)}, u32[]{:S(2)}) collective-permute-start(f32[1,128,256]{2,1,0:T(8,128)S(1)} %get-tuple-element.31), channel_id=1, source_target_pairs={{0,8},{8,16},{16,24},{24,0},{1,9},{9,17},{17,25},{25,1},{2,10},{10... | collective-permute-start | bytes 393224 | tf_op jit(solution)/shard_map/ppermute | solution.py:18
  69.5 4.7 %collective-permute-start.10 = (f32[1,128,256]{2,1,0:T(8,128)S(1)}, f32[1,128,256]{2,1,0:T(8,128)S(1)}, u32[]{:S(2)}, u32[]{:S(2)}) collective-permute-start(f32[1,128,256]{2,1,0:T(8,128)S(1)} %get-tuple-element.32), channel_id=1, source_target_pairs={{0,1},{1,2},{2,3},{3,4},{4,5},{5,6},{6,7},{7,0},{8,9},{9,10},{10,1... | collective-permute-start | bytes 393224 | tf_op jit(solution)/shard_map/ppermute | solution.py:18
  69.5 4.7 %collective-permute-start.11 = (f32[1,128,256]{2,1,0:T(8,128)S(1)}, f32[1,128,256]{2,1,0:T(8,128)S(1)}, u32[]{:S(2)}, u32[]{:S(2)}) collective-permute-start(f32[1,128,256]{2,1,0:T(8,128)S(1)} %get-tuple-element.33), channel_id=1, source_target_pairs={{1,0},{2,1},{3,2},{4,3},{5,4},{6,5},{7,6},{0,7},{9,8},{10,9},{11,1... | collective-permute-start | bytes 393224 | tf_op jit(solution)/shard_map/ppermute | solution.py:20
  71.6 5.9 %collective-permute-start.9 = (f32[1,128,256]{2,1,0:T(8,128)S(1)}, f32[1,128,256]{2,1,0:T(8,128)S(1)}, u32[]{:S(2)}, u32[]{:S(2)}) collective-permute-start(f32[1,128,256]{2,1,0:T(8,128)S(1)} %get-tuple-element.34), channel_id=1, source_target_pairs={{8,0},{16,8},{24,16},{0,24},{9,1},{17,9},{25,17},{1,25},{10,2},{18... | collective-permute-start | bytes 393224 | tf_op jit(solution)/shard_map/ppermute | solution.py:20
  159.1 5.3 %collective-permute-start.12 = (f32[1,128,256]{2,1,0:T(8,128)S(1)}, f32[1,128,256]{2,1,0:T(8,128)S(1)}, u32[]{:S(2)}, u32[]{:S(2)}) collective-permute-start(f32[1,128,256]{2,1,0:T(8,128)S(1)} %get-tuple-element.23), channel_id=1, source_target_pairs={{0,8},{8,16},{16,24},{24,0},{1,9},{9,17},{17,25},{25,1},{2,10},{10... | collective-permute-start | bytes 393224 | tf_op jit(solution)/shard_map/ppermute | solution.py:18
  160.6 4.4 %collective-permute-start.14 = (f32[1,128,256]{2,1,0:T(8,128)S(1)}, f32[1,128,256]{2,1,0:T(8,128)S(1)}, u32[]{:S(2)}, u32[]{:S(2)}) collective-permute-start(f32[1,128,256]{2,1,0:T(8,128)S(1)} %get-tuple-element.24), channel_id=1, source_target_pairs={{0,1},{1,2},{2,3},{3,4},{4,5},{5,6},{6,7},{7,0},{8,9},{9,10},{10,1... | collective-permute-start | bytes 393224 | tf_op jit(solution)/shard_map/ppermute | solution.py:18
  160.6 4.4 %collective-permute-start.15 = (f32[1,128,256]{2,1,0:T(8,128)S(1)}, f32[1,128,256]{2,1,0:T(8,128)S(1)}, u32[]{:S(2)}, u32[]{:S(2)}) collective-permute-start(f32[1,128,256]{2,1,0:T(8,128)S(1)} %get-tuple-element.25), channel_id=1, source_target_pairs={{1,0},{2,1},{3,2},{4,3},{5,4},{6,5},{7,6},{0,7},{9,8},{10,9},{11,1... | collective-permute-start | bytes 393224 | tf_op jit(solution)/shard_map/ppermute | solution.py:20
  162.3 5.9 %collective-permute-start.13 = (f32[1,128,256]{2,1,0:T(8,128)S(1)}, f32[1,128,256]{2,1,0:T(8,128)S(1)}, u32[]{:S(2)}, u32[]{:S(2)}) collective-permute-start(f32[1,128,256]{2,1,0:T(8,128)S(1)} %get-tuple-element.26), channel_id=1, source_target_pairs={{8,0},{16,8},{24,16},{0,24},{9,1},{17,9},{25,17},{1,25},{10,2},{18... | collective-permute-start | bytes 393224 | tf_op jit(solution)/shard_map/ppermute | solution.py:20
  178.6 5.8 %collective-permute-start.16 = (f32[1,128,256]{2,1,0:T(8,128)S(1)}, f32[1,128,256]{2,1,0:T(8,128)S(1)}, u32[]{:S(2)}, u32[]{:S(2)}) collective-permute-start(f32[1,128,256]{2,1,0:T(8,128)S(1)} %get-tuple-element.15), channel_id=1, source_target_pairs={{0,8},{8,16},{16,24},{24,0},{1,9},{9,17},{17,25},{25,1},{2,10},{10... | collective-permute-start | bytes 393224 | tf_op jit(solution)/shard_map/ppermute | solution.py:18
  179.2 5.2 %collective-permute-start.18 = (f32[1,128,256]{2,1,0:T(8,128)S(1)}, f32[1,128,256]{2,1,0:T(8,128)S(1)}, u32[]{:S(2)}, u32[]{:S(2)}) collective-permute-start(f32[1,128,256]{2,1,0:T(8,128)S(1)} %get-tuple-element.16), channel_id=1, source_target_pairs={{0,1},{1,2},{2,3},{3,4},{4,5},{5,6},{6,7},{7,0},{8,9},{9,10},{10,1... | collective-permute-start | bytes 393224 | tf_op jit(solution)/shard_map/ppermute | solution.py:18
  179.2 5.2 %collective-permute-start.19 = (f32[1,128,256]{2,1,0:T(8,128)S(1)}, f32[1,128,256]{2,1,0:T(8,128)S(1)}, u32[]{:S(2)}, u32[]{:S(2)}) collective-permute-start(f32[1,128,256]{2,1,0:T(8,128)S(1)} %get-tuple-element.17), channel_id=1, source_target_pairs={{1,0},{2,1},{3,2},{4,3},{5,4},{6,5},{7,6},{0,7},{9,8},{10,9},{11,1... | collective-permute-start | bytes 393224 | tf_op jit(solution)/shard_map/ppermute | solution.py:20
  181.3 5.9 %collective-permute-start.17 = (f32[1,128,256]{2,1,0:T(8,128)S(1)}, f32[1,128,256]{2,1,0:T(8,128)S(1)}, u32[]{:S(2)}, u32[]{:S(2)}) collective-permute-start(f32[1,128,256]{2,1,0:T(8,128)S(1)} %get-tuple-element.18), channel_id=1, source_target_pairs={{8,0},{16,8},{24,16},{0,24},{9,1},{17,9},{25,17},{1,25},{10,2},{18... | collective-permute-start | bytes 393224 | tf_op jit(solution)/shard_map/ppermute | solution.py:20
  189.5 47.2 %copy-start.1 = (f32[512,256]{1,0:T(8,128)S(1)}, f32[512,256]{1,0:T(8,128)}, u32[]{:S(2)}) copy-start(f32[512,256]{1,0:T(8,128)} %gather_fusion.9) | copy-start | bytes 1572868
where the time goes:
time: 238 us
  blocking collectives  152 us (64%)
  local copies, waits for them, and re-layouts  24.6 us (10%)
  waiting for transfers between devices  21.7 us (9%)
  starting transfers between devices  19.1 us (8%)
  matrix products  13 us (5%)
  other arithmetic  5.91 us (2%)
    psum x2, blocking collectives, on_device(): numerator = lax.psum(jnp.sum(residual * search, axis=0), ('gx', 'gy'))  91.8 us
    unnamed x2, blocking collectives  45 us
    all_gather x2, blocking collectives, coarse_by_column(): column_res = lax.all_gather(corner_res, 'gx', axis=0, tiled=True)  15.1 us
    ppermute x10, waiting for transfers between devices, with_halo(): lax.ppermute(head, axis, [((i + 1) % count, i) for i in range(count)])  13.5 us
    dot_general x10, matrix products, matmul(): jnp.dot(first_op, second_op, precision=highest, preferred_element_type=jn...  13 us
    ppermute x10, starting transfers between devices, with_halo(): lax.ppermute(head, axis, [((i + 1) % count, i) for i in range(count)])  12.9 us
    gather x5, local copies, waits for them, and re-layouts, edge_jumps(): jnp.take(source, local_rows, axis=0).reshape(4, edge_size, source.shape[1])  9.57 us
    gather x5, local copies, waits for them, and re-layouts, edge_jumps(): return jnp.take(stacked, inverse, axis=0)  8.53 us
  transfers between devices with their start and end apart: 20, of which 11 were waited for; matrix products, arithmetic and copies ran while one was open for 1% of the time, Pallas kernels for 0%

commit v1 on v0

--- a/solution.py
+++ b/solution.py
@@ -44,7 +44,14 @@
 def coarse_by_column(corner_res, coarse_inv, grid_row):
     across_count = lax.axis_size("gx")
     along_count = lax.axis_size("gy")
-    column_res = lax.all_gather(corner_res, "gx", axis=0, tiled=True)
+    size = lax.axis_size("gx")
+    right = [(i_2, (i_2 + 1) % size) for i_2 in range(size)]
+    blocks = [corner_res]
+    for far in range(1, size):
+        blocks = [lax.ppermute(blocks[0], "gx", right), *blocks]
+    out = jnp.concatenate(blocks, axis=0)
+    places = (lax.axis_index("gx") + 1) * blocks[-1].shape[0]
+    column_res = jnp.roll(out, places, axis=0)
     group_rows = coarse_inv.shape[0]
     shaped = coarse_inv.reshape(group_rows, across_count, along_count, MODES)
     chosen = lax.dynamic_slice_in_dim(shaped, grid_row, 1, 2).reshape(

time: 238 us -> 251 us (1.055)
  blocking collectives: 152 us -> 138 us
  waiting for transfers between devices: 21.7 us -> 35.1 us
  starting transfers between devices: 19.1 us -> 32.4 us
    all_gather x2 -> x0, blocking collectives: 15.1 us -> none  [coarse_by_column(): column_res = lax.all_gather(corner_res, 'gx', axis=0, tiled=True)]
    ppermute x0 -> x6, starting transfers between devices: none -> 11.6 us  [coarse_by_column(): blocks = [lax.ppermute(blocks[0], 'gx', right), *blocks]]
    ppermute x0 -> x6, waiting for transfers between devices: none -> 9.84 us  [coarse_by_column(): blocks = [lax.ppermute(blocks[0], 'gx', right), *blocks]]
    ppermute x10, waiting for transfers between devices: 8.15 us -> 11.7 us  [with_halo(): lax.ppermute(tail, axis, [(i, (i + 1) % count) for i in range(count)])]
  transfers between devices with their start and end apart: 20 -> 26, of which waited for: 11 -> 19; matrix products, arithmetic and copies ran while one was open for 1% -> 0% of each run, Pallas kernels for 0% -> 0%
where the time goes in v1:
time: 251 us
  blocking collectives  138 us (55%)
  waiting for transfers between devices  35.1 us (14%)
  starting transfers between devices  32.4 us (13%)
  local copies, waits for them, and re-layouts  24.5 us (10%)
  matrix products  13 us (5%)
  other arithmetic  5.89 us (2%)
    psum x2, blocking collectives, on_device(): numerator = lax.psum(jnp.sum(residual * search, axis=0), ('gx', 'gy'))  93.4 us
    unnamed x2, blocking collectives  44.8 us
    ppermute x10, waiting for transfers between devices, with_halo(): lax.ppermute(head, axis, [((i + 1) % count, i) for i in range(count)])  13.6 us
    ppermute x10, starting transfers between devices, with_halo(): lax.ppermute(head, axis, [((i + 1) % count, i) for i in range(count)])  13.2 us
    dot_general x10, matrix products, matmul(): jnp.dot(first_op, second_op, precision=highest, preferred_element_type=jn...  13 us
    ppermute x10, waiting for transfers between devices, with_halo(): lax.ppermute(tail, axis, [(i, (i + 1) % count) for i in range(count)])  11.7 us
    ppermute x6, starting transfers between devices, coarse_by_column(): blocks = [lax.ppermute(blocks[0], 'gx', right), *blocks]  11.6 us
    ppermute x6, waiting for transfers between devices, coarse_by_column(): blocks = [lax.ppermute(blocks[0], 'gx', right), *blocks]  9.84 us
  transfers between devices with their start and end apart: 26, of which 19 were waited for; matrix products, arithmetic and copies ran while one was open for 0% of the time, Pallas kernels for 0%

profile of v1, /device:TPU:10, one launch (start us, length us, event | category | flops | bytes accessed | tf_op | source)
XLA Modules:
  0.0 250.8 jit_solution(9769121495454574540)
XLA Ops:
  1.4 2.4 scatter_custom_fusion
  3.9 2.6 %gather_fusion = f32[512,256]{1,0:T(8,128)S(1)} fusion(f32[512,256]{1,0:T(8,128)} %bitcast.130, s32[1024]{0:T(1024)S(1)} %pad_clamp_fusion.1), kind=kCustom, calls=%fused_computation.clone | custom fusion | bytes 1050624 | tf_op jit(solution)/shard_map/jit(_take)/gather | solution.py:33
  8.3 1.7 collective-permute-start.3
  13.8 2.4 collective-permute-done.1
  19.6 3.0 %collective-permute-done.4 = f32[4,256]{1,0:T(4,128)S(1)} collective-permute-done((f32[4,256]{1,0:T(4,128)S(1)}, f32[4,256]{1,0:T(4,128)S(1)}, u32[]{:S(2)}, u32[]{:S(2)}) %collective-permute-start.4) | collective-permute-done | bytes 4128 | tf_op jit(solution)/shard_map/ppermute | solution.py:51
  24.2 2.0 collective-permute-done.5
  26.2 2.4 collective-permute-start.6
  30.7 23.8 %all-reduce = f32[32,256]{1,0:T(8,128)S(1)} all-reduce(f32[32,256]{1,0:T(8,128)S(1)} %fusion.35), channel_id=2, replica_groups=mesh['gx'=4,'gy'=8] {'gy'}, use_global_device_ids=true, to_apply=%region_1.4.clone | all-reduce | flops 8192 | bytes 65536
  55.0 2.0 fusion.2
  58.9 2.7 %collective-permute-start.7 = (f32[1,128,256]{2,1,0:T(8,128)S(1)}, f32[1,128,256]{2,1,0:T(8,128)S(1)}, u32[]{:S(2)}, u32[]{:S(2)}) collective-permute-start(f32[1,128,256]{2,1,0:T(8,128)S(1)} %get-tuple-element.40), channel_id=1, source_target_pairs={{0,8},{8,16},{16,24},{24,0},{1,9},{9,17},{17,25},{25,1},{2,10},{10... | collective-permute-start | bytes 393224 | tf_op jit(solution)/shard_map/ppermute | solution.py:18
  63.3 2.0 collective-permute-done.7
  66.0 3.2 %collective-permute-done.8 = f32[1,128,256]{2,1,0:T(8,128)S(1)} collective-permute-done((f32[1,128,256]{2,1,0:T(8,128)S(1)}, f32[1,128,256]{2,1,0:T(8,128)S(1)}, u32[]{:S(2)}, u32[]{:S(2)}) %collective-permute-start.8) | collective-permute-done | bytes 131104 | tf_op jit(solution)/shard_map/ppermute | solution.py:20
  70.9 3.2 %convolution_bitcast_fusion.1 = f32[512,256]{0,1:T(8,128)S(1)} fusion(f32[1,1,512,512]{3,2,1,0:T(8,128)} %param.10, f32[512,256]{1,0:T(8,128)S(1)} %gather_fusion.3, pred[512]{0:T(512)(128)(4,1)S(1)} %get-tuple-element.56), kind=kOutput, calls=%fused_computation.18 | convolution fusion | flops 805437440 | bytes 2097664 | tf_op jit(solution)/shard_map/dot_general | solution.py:28
  76.2 1.8 collective-permute-start.14
  78.0 1.9 collective-permute-start.12
  79.9 2.2 collective-permute-done.11
  82.1 1.8 collective-permute-done.12
  85.7 46.7 %all-reduce.3 = (f32[256]{0:T(256)S(1)}, f32[256]{0:T(256)S(1)}) all-reduce(f32[256]{0:T(256)S(1)} %get-tuple-element.7, f32[256]{0:T(256)S(1)} %get-tuple-element.6), channel_id=1, replica_groups=mesh['gx'=4,'gy'=8] {'gx','gy'}, use_global_device_ids=true, to_apply=%region_3.6 | all-reduce | flops 512 | bytes 4096 | tf_op jit(solution)/shard_map/psum | solution.py:83
  134.4 2.2 collective-permute-done.15
  136.5 2.4 collective-permute-start.16
  140.2 3.2 %collective-permute-start.17 = (f32[4,256]{1,0:T(4,128)S(1)}, f32[4,256]{1,0:T(4,128)S(1)}, u32[]{:S(2)}, u32[]{:S(2)}) collective-permute-start(f32[4,256]{1,0:T(4,128)S(1)} %collective-permute-done.16), channel_id=1, source_target_pairs={{0,8},{8,16},{16,24},{24,0},{1,9},{9,17},{17,25},{25,1},{2,10},{10... | collective-permute-start | bytes 12296 | tf_op jit(solution)/shard_map/ppermute | solution.py:51
  144.9 21.0 %all-reduce.1 = f32[32,256]{1,0:T(8,128)S(1)} all-reduce(f32[32,256]{1,0:T(8,128)S(1)} %fusion.25), channel_id=3, replica_groups=mesh['gx'=4,'gy'=8] {'gy'}, use_global_device_ids=true, to_apply=%region_6.9.clone | all-reduce | flops 8192 | bytes 65536
  166.4 1.9 fusion.3
  170.3 3.2 %collective-permute-start.18 = (f32[1,128,256]{2,1,0:T(8,128)S(1)}, f32[1,128,256]{2,1,0:T(8,128)S(1)}, u32[]{:S(2)}, u32[]{:S(2)}) collective-permute-start(f32[1,128,256]{2,1,0:T(8,128)S(1)} %get-tuple-element.24), channel_id=1, source_target_pairs={{0,8},{8,16},{16,24},{24,0},{1,9},{9,17},{17,25},{25,1},{2,10},{10... | collective-permute-start | bytes 393224 | tf_op jit(solution)/shard_map/ppermute | solution.py:18
  175.2 2.0 collective-permute-done.18
  177.9 3.2 %collective-permute-done.19 = f32[1,128,256]{2,1,0:T(8,128)S(1)} collective-permute-done((f32[1,128,256]{2,1,0:T(8,128)S(1)}, f32[1,128,256]{2,1,0:T(8,128)S(1)}, u32[]{:S(2)}, u32[]{:S(2)}) %collective-permute-start.19) | collective-permute-done | bytes 131104 | tf_op jit(solution)/shard_map/ppermute | solution.py:20
  182.8 4.0 %convolution_bitcast_fusion = f32[512,256]{0,1:T(8,128)} fusion(f32[1,1,512,512]{3,2,1,0:T(8,128)} %param.10, f32[512,256]{1,0:T(8,128)S(1)} %gather_fusion.7, pred[512]{0:T(512)(128)(4,1)S(1)} %get-tuple-element.56), kind=kOutput, calls=%fused_computation.17 | convolution fusion | flops 805437440 | bytes 2097664 | tf_op jit(solution)/shard_map/dot_general | solution.py:28
  188.0 2.2 gather_fusion.8
  193.3 2.0 collective-permute-start.23
  195.3 2.2 collective-permute-done.22
  199.3 2.2 gather_fusion.9
  202.9 46.7 %all-reduce.2 = (f32[256]{0:T(256)S(1)}, f32[256]{0:T(256)S(1)}) all-reduce(f32[256]{0:T(256)S(1)} %get-tuple-element.5, f32[256]{0:T(256)S(1)} %get-tuple-element.4), channel_id=1, replica_groups=mesh['gx'=4,'gy'=8] {'gx','gy'}, use_global_device_ids=true, to_apply=%region_8.11 | all-reduce | flops 512 | bytes 4096 | tf_op jit(solution)/shard_map/psum | solution.py:83
  (96 shorter events, 43.1 us)
Async XLA Ops:
  0.6 54.4 %copy-start = (f32[1,1,512,512]{3,2,1,0:T(8,128)S(1)}, f32[1,1,512,512]{3,2,1,0:T(8,128)}, u32[]{:S(2)}) copy-start(f32[1,1,512,512]{3,2,1,0:T(8,128)} %param.11) | copy-start | bytes 3145732
  1.4 2.4 copy-start.2
  6.7 5.3 %collective-permute-start = (f32[1,128,256]{2,1,0:T(8,128)S(1)}, f32[1,128,256]{2,1,0:T(8,128)S(1)}, u32[]{:S(2)}, u32[]{:S(2)}) collective-permute-start(f32[1,128,256]{2,1,0:T(8,128)S(1)} %get-tuple-element.48), channel_id=1, source_target_pairs={{0,8},{8,16},{16,24},{24,0},{1,9},{9,17},{17,25},{25,1},{2,10},{10... | collective-permute-start | bytes 393224 | tf_op jit(solution)/shard_map/ppermute | solution.py:18
  8.3 4.4 %collective-permute-start.2 = (f32[1,128,256]{2,1,0:T(8,128)S(1)}, f32[1,128,256]{2,1,0:T(8,128)S(1)}, u32[]{:S(2)}, u32[]{:S(2)}) collective-permute-start(f32[1,128,256]{2,1,0:T(8,128)S(1)} %get-tuple-element.49), channel_id=1, source_target_pairs={{0,1},{1,2},{2,3},{3,4},{4,5},{5,6},{6,7},{7,0},{8,9},{9,10},{10,1... | collective-permute-start | bytes 393224 | tf_op jit(solution)/shard_map/ppermute | solution.py:18
  8.3 5.6 %collective-permute-start.3 = (f32[1,128,256]{2,1,0:T(8,128)S(1)}, f32[1,128,256]{2,1,0:T(8,128)S(1)}, u32[]{:S(2)}, u32[]{:S(2)}) collective-permute-start(f32[1,128,256]{2,1,0:T(8,128)S(1)} %get-tuple-element.50), channel_id=1, source_target_pairs={{1,0},{2,1},{3,2},{4,3},{5,4},{6,5},{7,6},{0,7},{9,8},{10,9},{11,1... | collective-permute-start | bytes 393224 | tf_op jit(solution)/shard_map/ppermute | solution.py:20
  10.0 6.2 %collective-permute-start.1 = (f32[1,128,256]{2,1,0:T(8,128)S(1)}, f32[1,128,256]{2,1,0:T(8,128)S(1)}, u32[]{:S(2)}, u32[]{:S(2)}) collective-permute-start(f32[1,128,256]{2,1,0:T(8,128)S(1)} %get-tuple-element.51), channel_id=1, source_target_pairs={{8,0},{16,8},{24,16},{0,24},{9,1},{17,9},{25,17},{1,25},{10,2},{18... | collective-permute-start | bytes 393224 | tf_op jit(solution)/shard_map/ppermute | solution.py:20
  18.0 0.7 copy-start.4
  18.6 5.5 %copy-start.3 = (f32[32,128]{1,0:T(8,128)S(1)}, f32[32,128]{1,0:T(8,128)}, u32[]{:S(2)}) copy-start(f32[32,128]{1,0:T(8,128)} %param.13) | copy-start | bytes 49156
  19.0 3.7 %collective-permute-start.4 = (f32[4,256]{1,0:T(4,128)S(1)}, f32[4,256]{1,0:T(4,128)S(1)}, u32[]{:S(2)}, u32[]{:S(2)}) collective-permute-start(f32[4,256]{1,0:T(4,128)S(1)} %fusion.10), channel_id=1, source_target_pairs={{0,8},{8,16},{16,24},{24,0},{1,9},{9,17},{17,25},{25,1},{2,10},{10... | collective-permute-start | bytes 12296 | tf_op jit(solution)/shard_map/ppermute | solution.py:51
  22.6 3.6 %collective-permute-start.5 = (f32[4,256]{1,0:T(4,128)S(1)}, f32[4,256]{1,0:T(4,128)S(1)}, u32[]{:S(2)}, u32[]{:S(2)}) collective-permute-start(f32[4,256]{1,0:T(4,128)S(1)} %collective-permute-done.4), channel_id=1, source_target_pairs={{0,8},{8,16},{16,24},{24,0},{1,9},{9,17},{17,25},{25,1},{2,10},{10... | collective-permute-start | bytes 12296 | tf_op jit(solution)/shard_map/ppermute | solution.py:51
  26.2 4.3 %collective-permute-start.6 = (f32[4,256]{1,0:T(4,128)S(1)}, f32[4,256]{1,0:T(4,128)S(1)}, u32[]{:S(2)}, u32[]{:S(2)}) collective-permute-start(f32[4,256]{1,0:T(4,128)S(1)} %collective-permute-done.5), channel_id=1, source_target_pairs={{0,8},{8,16},{16,24},{24,0},{1,9},{9,17},{17,25},{25,1},{2,10},{10... | collective-permute-start | bytes 12296 | tf_op jit(solution)/shard_map/ppermute | solution.py:51
  28.6 0.7 copy-start.5
  58.9 6.4 %collective-permute-start.7 = (f32[1,128,256]{2,1,0:T(8,128)S(1)}, f32[1,128,256]{2,1,0:T(8,128)S(1)}, u32[]{:S(2)}, u32[]{:S(2)}) collective-permute-start(f32[1,128,256]{2,1,0:T(8,128)S(1)} %get-tuple-element.40), channel_id=1, source_target_pairs={{0,8},{8,16},{16,24},{24,0},{1,9},{9,17},{17,25},{25,1},{2,10},{10... | collective-permute-start | bytes 393224 | tf_op jit(solution)/shard_map/ppermute | solution.py:18
  61.6 4.4 %collective-permute-start.9 = (f32[1,128,256]{2,1,0:T(8,128)S(1)}, f32[1,128,256]{2,1,0:T(8,128)S(1)}, u32[]{:S(2)}, u32[]{:S(2)}) collective-permute-start(f32[1,128,256]{2,1,0:T(8,128)S(1)} %get-tuple-element.41), channel_id=1, source_target_pairs={{0,1},{1,2},{2,3},{3,4},{4,5},{5,6},{6,7},{7,0},{8,9},{9,10},{10,1... | collective-permute-start | bytes 393224 | tf_op jit(solution)/shard_map/ppermute | solution.py:18
  61.6 4.4 %collective-permute-start.10 = (f32[1,128,256]{2,1,0:T(8,128)S(1)}, f32[1,128,256]{2,1,0:T(8,128)S(1)}, u32[]{:S(2)}, u32[]{:S(2)}) collective-permute-start(f32[1,128,256]{2,1,0:T(8,128)S(1)} %get-tuple-element.42), channel_id=1, source_target_pairs={{1,0},{2,1},{3,2},{4,3},{5,4},{6,5},{7,6},{0,7},{9,8},{10,9},{11,1... | collective-permute-start | bytes 393224 | tf_op jit(solution)/shard_map/ppermute | solution.py:20
  63.3 5.9 %collective-permute-start.8 = (f32[1,128,256]{2,1,0:T(8,128)S(1)}, f32[1,128,256]{2,1,0:T(8,128)S(1)}, u32[]{:S(2)}, u32[]{:S(2)}) collective-permute-start(f32[1,128,256]{2,1,0:T(8,128)S(1)} %get-tuple-element.43), channel_id=1, source_target_pairs={{8,0},{16,8},{24,16},{0,24},{9,1},{17,9},{25,17},{1,25},{10,2},{18... | collective-permute-start | bytes 393224 | tf_op jit(solution)/shard_map/ppermute | solution.py:20
  76.1 6.0 %collective-permute-start.11 = (f32[1,128,256]{2,1,0:T(8,128)S(1)}, f32[1,128,256]{2,1,0:T(8,128)S(1)}, u32[]{:S(2)}, u32[]{:S(2)}) collective-permute-start(f32[1,128,256]{2,1,0:T(8,128)S(1)} %get-tuple-element.32), channel_id=1, source_target_pairs={{0,8},{8,16},{16,24},{24,0},{1,9},{9,17},{17,25},{25,1},{2,10},{10... | collective-permute-start | bytes 393224 | tf_op jit(solution)/shard_map/ppermute | solution.py:18
  76.1 5.9 %collective-permute-start.13 = (f32[1,128,256]{2,1,0:T(8,128)S(1)}, f32[1,128,256]{2,1,0:T(8,128)S(1)}, u32[]{:S(2)}, u32[]{:S(2)}) collective-permute-start(f32[1,128,256]{2,1,0:T(8,128)S(1)} %get-tuple-element.33), channel_id=1, source_target_pairs={{0,1},{1,2},{2,3},{3,4},{4,5},{5,6},{6,7},{7,0},{8,9},{9,10},{10,1... | collective-permute-start | bytes 393224 | tf_op jit(solution)/shard_map/ppermute | solution.py:18
  76.2 5.9 %collective-permute-start.14 = (f32[1,128,256]{2,1,0:T(8,128)S(1)}, f32[1,128,256]{2,1,0:T(8,128)S(1)}, u32[]{:S(2)}, u32[]{:S(2)}) collective-permute-start(f32[1,128,256]{2,1,0:T(8,128)S(1)} %get-tuple-element.34), channel_id=1, source_target_pairs={{1,0},{2,1},{3,2},{4,3},{5,4},{6,5},{7,6},{0,7},{9,8},{10,9},{11,1... | collective-permute-start | bytes 393224 | tf_op jit(solution)/shard_map/ppermute | solution.py:20
  78.0 5.9 %collective-permute-start.12 = (f32[1,128,256]{2,1,0:T(8,128)S(1)}, f32[1,128,256]{2,1,0:T(8,128)S(1)}, u32[]{:S(2)}, u32[]{:S(2)}) collective-permute-start(f32[1,128,256]{2,1,0:T(8,128)S(1)} %get-tuple-element.35), channel_id=1, source_target_pairs={{8,0},{16,8},{24,16},{0,24},{9,1},{17,9},{25,17},{1,25},{10,2},{18... | collective-permute-start | bytes 393224 | tf_op jit(solution)/shard_map/ppermute | solution.py:20
  132.8 3.7 %collective-permute-start.15 = (f32[4,256]{1,0:T(4,128)S(1)}, f32[4,256]{1,0:T(4,128)S(1)}, u32[]{:S(2)}, u32[]{:S(2)}) collective-permute-start(f32[4,256]{1,0:T(4,128)S(1)} %fusion.42), channel_id=1, source_target_pairs={{0,8},{8,16},{16,24},{24,0},{1,9},{9,17},{17,25},{25,1},{2,10},{10... | collective-permute-start | bytes 12296 | tf_op jit(solution)/shard_map/ppermute | solution.py:51
  136.5 3.7 %collective-permute-start.16 = (f32[4,256]{1,0:T(4,128)S(1)}, f32[4,256]{1,0:T(4,128)S(1)}, u32[]{:S(2)}, u32[]{:S(2)}) collective-permute-start(f32[4,256]{1,0:T(4,128)S(1)} %collective-permute-done.15), channel_id=1, source_target_pairs={{0,8},{8,16},{16,24},{24,0},{1,9},{9,17},{17,25},{25,1},{2,10},{10... | collective-permute-start | bytes 12296 | tf_op jit(solution)/shard_map/ppermute | solution.py:51
  140.2 4.5 %collective-permute-start.17 = (f32[4,256]{1,0:T(4,128)S(1)}, f32[4,256]{1,0:T(4,128)S(1)}, u32[]{:S(2)}, u32[]{:S(2)}) collective-permute-start(f32[4,256]{1,0:T(4,128)S(1)} %collective-permute-done.16), channel_id=1, source_target_pairs={{0,8},{8,16},{16,24},{24,0},{1,9},{9,17},{17,25},{25,1},{2,10},{10... | collective-permute-start | bytes 12296 | tf_op jit(solution)/shard_map/ppermute | solution.py:51
  170.3 6.9 %collective-permute-start.18 = (f32[1,128,256]{2,1,0:T(8,128)S(1)}, f32[1,128,256]{2,1,0:T(8,128)S(1)}, u32[]{:S(2)}, u32[]{:S(2)}) collective-permute-start(f32[1,128,256]{2,1,0:T(8,128)S(1)} %get-tuple-element.24), channel_id=1, source_target_pairs={{0,8},{8,16},{16,24},{24,0},{1,9},{9,17},{17,25},{25,1},{2,10},{10... | collective-permute-start | bytes 393224 | tf_op jit(solution)/shard_map/ppermute | solution.py:18
  173.5 4.4 %collective-permute-start.20 = (f32[1,128,256]{2,1,0:T(8,128)S(1)}, f32[1,128,256]{2,1,0:T(8,128)S(1)}, u32[]{:S(2)}, u32[]{:S(2)}) collective-permute-start(f32[1,128,256]{2,1,0:T(8,128)S(1)} %get-tuple-element.25), channel_id=1, source_target_pairs={{0,1},{1,2},{2,3},{3,4},{4,5},{5,6},{6,7},{7,0},{8,9},{9,10},{10,1... | collective-permute-start | bytes 393224 | tf_op jit(solution)/shard_map/ppermute | solution.py:18
  173.5 4.4 %collective-permute-start.21 = (f32[1,128,256]{2,1,0:T(8,128)S(1)}, f32[1,128,256]{2,1,0:T(8,128)S(1)}, u32[]{:S(2)}, u32[]{:S(2)}) collective-permute-start(f32[1,128,256]{2,1,0:T(8,128)S(1)} %get-tuple-element.26), channel_id=1, source_target_pairs={{1,0},{2,1},{3,2},{4,3},{5,4},{6,5},{7,6},{0,7},{9,8},{10,9},{11,1... | collective-permute-start | bytes 393224 | tf_op jit(solution)/shard_map/ppermute | solution.py:20
  175.2 5.9 %collective-permute-start.19 = (f32[1,128,256]{2,1,0:T(8,128)S(1)}, f32[1,128,256]{2,1,0:T(8,128)S(1)}, u32[]{:S(2)}, u32[]{:S(2)}) collective-permute-start(f32[1,128,256]{2,1,0:T(8,128)S(1)} %get-tuple-element.27), channel_id=1, source_target_pairs={{8,0},{16,8},{24,16},{0,24},{9,1},{17,9},{25,17},{1,25},{10,2},{18... | collective-permute-start | bytes 393224 | tf_op jit(solution)/shard_map/ppermute | solution.py:20
  191.5 6.0 %collective-permute-start.22 = (f32[1,128,256]{2,1,0:T(8,128)S(1)}, f32[1,128,256]{2,1,0:T(8,128)S(1)}, u32[]{:S(2)}, u32[]{:S(2)}) collective-permute-start(f32[1,128,256]{2,1,0:T(8,128)S(1)} %get-tuple-element.16), channel_id=1, source_target_pairs={{0,8},{8,16},{16,24},{24,0},{1,9},{9,17},{17,25},{25,1},{2,10},{10... | collective-permute-start | bytes 393224 | tf_op jit(solution)/shard_map/ppermute | solution.py:18
  191.5 5.9 %collective-permute-start.24 = (f32[1,128,256]{2,1,0:T(8,128)S(1)}, f32[1,128,256]{2,1,0:T(8,128)S(1)}, u32[]{:S(2)}, u32[]{:S(2)}) collective-permute-start(f32[1,128,256]{2,1,0:T(8,128)S(1)} %get-tuple-element.17), channel_id=1, source_target_pairs={{0,1},{1,2},{2,3},{3,4},{4,5},{5,6},{6,7},{7,0},{8,9},{9,10},{10,1... | collective-permute-start | bytes 393224 | tf_op jit(solution)/shard_map/ppermute | solution.py:18
  191.6 5.9 %collective-permute-start.25 = (f32[1,128,256]{2,1,0:T(8,128)S(1)}, f32[1,128,256]{2,1,0:T(8,128)S(1)}, u32[]{:S(2)}, u32[]{:S(2)}) collective-permute-start(f32[1,128,256]{2,1,0:T(8,128)S(1)} %get-tuple-element.18), channel_id=1, source_target_pairs={{1,0},{2,1},{3,2},{4,3},{5,4},{6,5},{7,6},{0,7},{9,8},{10,9},{11,1... | collective-permute-start | bytes 393224 | tf_op jit(solution)/shard_map/ppermute | solution.py:20
  193.3 5.9 %collective-permute-start.23 = (f32[1,128,256]{2,1,0:T(8,128)S(1)}, f32[1,128,256]{2,1,0:T(8,128)S(1)}, u32[]{:S(2)}, u32[]{:S(2)}) collective-permute-start(f32[1,128,256]{2,1,0:T(8,128)S(1)} %get-tuple-element.19), channel_id=1, source_target_pairs={{8,0},{16,8},{24,16},{0,24},{9,1},{17,9},{25,17},{1,25},{10,2},{18... | collective-permute-start | bytes 393224 | tf_op jit(solution)/shard_map/ppermute | solution.py:20
  201.6 48.0 %copy-start.1 = (f32[512,256]{1,0:T(8,128)S(1)}, f32[512,256]{1,0:T(8,128)}, u32[]{:S(2)}) copy-start(f32[512,256]{1,0:T(8,128)} %gather_fusion.9) | copy-start | bytes 1572868
